TPU v7x, 32 devices: a whole 2x2x4 slice. The times are simulated.
32 devices in a mesh: req: 16 (over z, y, core), tp: 2 (over x).
Axes of the slice: x: 2, y: 2, z: 4, core: 2. Of those that a mesh axis runs over, the one named last changes fastest.
Arguments:
- queries: bfloat16 [96, 24, 8192], P('req', None, 'tp'), may hold values from -8 to 8
- fresh_kv: bfloat16 [96, 24, 2048], P('req', None, 'tp'), may hold values from -8 to 8
- key_value_pages: bfloat16 [832, 128, 2048], P('req', None, 'tp'), may hold values from -6 to 6
- cache_lengths: int32 [96], P('req'), may hold values from 1 to 4096, as said below
- page_table: int32 [96, 32], P('req'), may hold values from 0 to 51, as said below
- movers: int32 [16, 2], P('req'), may hold values from 0 to 5, as said below
- w_out: bfloat16 [4096, 8192], P('req', 'tp'), may hold values from -0.0625 to 0.0625
Outputs:
- projected: bfloat16 [2304, 4096], P('req', 'tp')
Inputs may be any that keep to these rules, and one draw needn't show every extreme that they name: `cache_lengths`: in every draw one request holds exactly 4096 positions. `cache_lengths`: A request in a slot named by movers holds at most 512 positions, and in every draw one of them holds exactly that many. `page_table`: the entries that a request's length uses are distinct pages among all requests of its owner; the other entries are any pages of the pool. `movers`: the two slots of a row differ.
All inputs are finite; a program needn't handle non-finite values.
Results may differ from a plain program's by a relative error of at most 0.0057.
Values may be sent and summed in bfloat16 or wider, within the bound.
A program may use at most 320 MiB of HBM per device.

v0:
```python
import jax
import jax.numpy as jnp
from jax import lax
from jax.sharding import PartitionSpec as P

HEAD_SIZE = 128
MIGP = 4


masked_score = -1e30


def passed_along(block, axis, distance):
    devices = range(lax.axis_size(axis))
    route = [((i - distance) % len(devices), i) for i in devices]
    return lax.ppermute(block, axis, route)


def attend(queries, fresh_kv, page_list, lengths):
    slots, token_count, width = queries.shape
    head_dim = HEAD_SIZE
    kv_heads = fresh_kv.shape[2] // (2 * head_dim)
    group = width // (kv_heads * head_dim)
    cached_rows = page_list.shape[1] * page_list.shape[2]
    cache_block = page_list.reshape(slots, cached_rows, kv_heads, 2 * head_dim)
    newer_rows = fresh_kv.reshape(slots, token_count, kv_heads, 2 * head_dim)
    cache_keys = cache_block[..., :head_dim]
    cache_values = cache_block[..., head_dim:]
    newer_keys = newer_rows[..., :head_dim]
    newer_values = newer_rows[..., head_dim:]
    query_head_rows = queries.reshape(slots, token_count, kv_heads, group, head_dim)
    scale = head_dim ** (-0.5)
    cache_scores = (
        jnp.einsum(
            "sqkgd,sckd->skgqc", query_head_rows, cache_keys, preferred_element_type=jnp.float32
        )
        * scale
    )
    newer_scores = (
        jnp.einsum(
            "sqkgd,sckd->skgqc", query_head_rows, newer_keys, preferred_element_type=jnp.float32
        )
        * scale
    )
    cache_pos = jnp.arange(cached_rows, dtype=jnp.int32)[None, None, :]
    cache_valid = cache_pos < lengths[:, None, None]
    newer_pos = jnp.arange(token_count, dtype=jnp.int32)[None, :]
    token_row = jnp.arange(token_count, dtype=jnp.int32)[:, None]
    newer_valid = newer_pos <= token_row
    cache_scores = jnp.where(cache_valid[:, None, None], cache_scores, masked_score)
    newer_scores = jnp.where(newer_valid[None, None, None], newer_scores, masked_score)
    highest = jnp.maximum(
        jnp.max(cache_scores, axis=-1, keepdims=True), jnp.max(newer_scores, axis=-1, keepdims=True)
    )
    cache_powers = jnp.exp(cache_scores - highest)
    newer_powers = jnp.exp(newer_scores - highest)
    total = jnp.sum(cache_powers, axis=-1, keepdims=True) + jnp.sum(
        newer_powers, axis=-1, keepdims=True
    )
    cache_weights = (cache_powers / total).astype(jnp.bfloat16)
    newer_weights = (newer_powers / total).astype(jnp.bfloat16)
    mixed = jnp.einsum(
        "skgqc,sckd->sqkgd", cache_weights, cache_values, preferred_element_type=jnp.float32
    )
    mixed = mixed + jnp.einsum(
        "skgqc,sckd->sqkgd", newer_weights, newer_values, preferred_element_type=jnp.float32
    )
    return mixed.astype(jnp.bfloat16).reshape(slots, token_count, width)


def per_device(queries, fresh_kv, key_value_pages, cache_lengths, page_table, movers, w_out):
    slots = queries.shape[0]
    slot_ids = jnp.arange(slots, dtype=jnp.int32)
    to_next = movers[0, 0]
    to_prev = movers[0, 1]
    moving = ((slot_ids == to_next) | (slot_ids == to_prev)).astype(jnp.int32)
    stayers = jnp.argsort(slot_ids + slots * moving)[: slots - 2]
    kept = attend(
        queries[stayers],
        fresh_kv[stayers],
        key_value_pages[page_table[stayers]],
        cache_lengths[stayers],
    )
    next_pages = key_value_pages[page_table[to_next, :MIGP]]
    prev_pages = key_value_pages[page_table[to_prev, :MIGP]]
    from_left = passed_along(
        (next_pages, queries[to_next], fresh_kv[to_next], cache_lengths[to_next][None]), "req", 1
    )
    from_right = passed_along(
        (prev_pages, queries[to_prev], fresh_kv[to_prev], cache_lengths[to_prev][None]), "req", -1
    )
    arrived = attend(
        jnp.stack([from_left[1], from_right[1]]),
        jnp.stack([from_left[2], from_right[2]]),
        jnp.stack([from_left[0], from_right[0]]),
        jnp.concatenate([from_left[3], from_right[3]]),
    )
    placed = jnp.zeros_like(queries).at[stayers].set(kept)
    placed = placed.at[to_next].set(arrived[0]).at[to_prev].set(arrived[1])
    flat = placed.reshape(slots * placed.shape[1], placed.shape[2])
    partial_sum = lax.dot_general(
        flat,
        lax.all_gather(w_out, "req", axis=0, tiled=True),
        (((1,), (1,)), ((), ())),
        preferred_element_type=jnp.float32,
    )
    return lax.psum_scatter(partial_sum, "tp", scatter_dimension=1, tiled=True).astype(jnp.bfloat16)


def solution(mesh):
    return jax.shard_map(
        per_device,
        mesh=mesh,
        in_specs=(
            P("req", None, "tp"),
            P("req", None, "tp"),
            P("req", None, "tp"),
            P("req"),
            P("req", None),
            P("req", None),
            P("req", "tp"),
        ),
        out_specs=P("req", "tp"),
        check_vma=False,
    )
```

profile of v0, /device:TPU:0, one launch (start us, length us, event | category | flops | bytes accessed | tf_op | source)
XLA Modules:
  0.0 316.9 jit_solution(2329500117669857769)
XLA Ops:
  6.5 0.7 all-gather.2.cloned.1.call-update
  7.3 1.4 fusion.33
  12.4 1.3 fusion.32
  13.8 0.5 collective-permute-start.2
  14.2 5.0 %collective-permute-start.3 = (s32[1]{0:T(128)}, s32[1]{0:T(128)}, u32[]{:S(2)}, u32[]{:S(2)}) collective-permute-start(s32[1]{0:T(128)} %get-tuple-element.46), channel_id=1, source_target_pairs={{2,0},{4,2},{6,4},{8,6},{10,8},{12,10},{14,12},{16,14},{18,16},{20... | collective-permute-start | bytes 20 | tf_op jit(solution)/shard_map/ppermute | solution.py:16
  19.2 0.8 fusion.24
  20.0 6.5 %gather_fusion.5 = bf16[4,128,1024]{2,1,0:T(8,128)(2,1)} fusion(bf16[52,128,1024]{2,1,0:T(8,128)(2,1)} %param.13, s32[1024]{0:T(1024)S(1)} %pad_clamp_fusion.1), kind=kCustom, calls=%fused_computation.5 | custom fusion | bytes 2097168 | tf_op jit(solution)/shard_map/gather | solution.py:84
  26.5 6.8 %gather_fusion.6 = bf16[4,128,1024]{2,1,0:T(8,128)(2,1)} fusion(bf16[52,128,1024]{2,1,0:T(8,128)(2,1)} %param.13, s32[1024]{0:T(1024)S(1)} %pad_clamp_fusion), kind=kCustom, calls=%fused_computation.6 | custom fusion | bytes 2097168 | tf_op jit(solution)/shard_map/gather | solution.py:85
  33.3 4.1 %collective-permute-start.1 = (bf16[4,128,1024]{2,1,0:T(8,128)(2,1)}, bf16[4,128,1024]{2,1,0:T(8,128)(2,1)}, u32[]{:S(2)}, u32[]{:S(2)}) collective-permute-start(bf16[4,128,1024]{2,1,0:T(8,128)(2,1)} %gather_fusion.6), channel_id=1, source_target_pairs={{2,0},{4,2},{6,4},{8,6},{10,8},{12,10},{14,12},{16,14},{18,16},{20... | collective-permute-start | bytes 3145736 | tf_op jit(solution)/shard_map/ppermute | solution.py:16
  37.5 0.8 dynamic-slice_bitcast_fusion
  38.3 1.2 fusion.20
  39.5 1.0 sort.17
  40.5 0.6 copy-done.10
  41.1 0.6 gather_fusion.2
  41.7 0.6 gather_fusion
  42.3 0.6 gather_fusion.3
  43.0 17.9 %gather_fusion.1 = bf16[128,128,1024]{2,1,0:T(8,128)(2,1)} fusion(bf16[52,128,1024]{2,1,0:T(8,128)(2,1)} %param.13, s32[1024]{0:T(1024)S(1)} %pad_clamp_fusion.2), kind=kCustom, calls=%fused_computation.1 | custom fusion | bytes 67109376 | tf_op jit(solution)/shard_map/gather | solution.py:81
  60.9 55.0 %reshape.245 = bf16[4,4096,4,256]{3,2,1,0:T(4,128)(2,1)} reshape(bf16[128,128,1024]{2,1,0:T(8,128)(2,1)} %gather_fusion.1) | data formatting | bytes 67108864 | tf_op jit(solution)/shard_map/reshape | solution.py:25
  116.0 0.6 gather_fusion.4
  116.8 1.4 fusion.34
  118.4 23.8 %fusion.29 = (bf16[4,4096,4,128]{3,2,1,0:T(4,128)(2,1)}, bf16[4,4096,4,128]{3,2,1,0:T(4,128)(2,1)}) fusion(bf16[4,4096,4,256]{3,2,1,0:T(4,128)(2,1)} %reshape.245), kind=kLoop, calls=%fused_computation.93 | loop fusion | bytes 67108864 | tf_op jit(solution)/shard_map/slice | solution.py:28
  142.1 35.6 %bitcast_reduce_fusion = (f32[4,4,8,24]{3,2,1,0:T(8,128)S(1)}, f32[4,4,4096,24,8]{2,3,4,1,0:T(8,128)}) fusion(pred[4,4096]{1,0:T(4,128)(4,1)S(1)} %iota_compare_fusion, bf16[4,24,4,8,128]{4,3,2,1,0:T(8,128)(2,1)S(1)} %bitcast.148, bf16[4,4096,4,128]{3,2,1,0:T(4,128)(2,1)} %get-tuple-element.34), kind=kOutput, calls=%fused_computation.9 | convolution fusion | flops 3258971136 | bytes 67923968 | tf_op jit(solution)/shard_map/sqkgd,sckd->skgqc/dot_general | solution.py:34
  177.8 0.5 fusion.7
  178.2 21.8 %fusion.1 = f32[4,4,8,24]{3,2,1,0:T(8,128)S(1)} fusion(f32[4,4,4096,24,8]{2,3,4,1,0:T(8,128)} %get-tuple-element.50, f32[4,4,8,24]{3,2,1,0:T(8,128)S(1)} %max.16, pred[4,4096]{1,0:T(4,128)(4,1)S(1)} %iota_compare_fusion), kind=kLoop, calls=%fused_computation.13 | loop fusion | flops 50328576 | bytes 50372608 | tf_op jit(solution)/shard_map/reduce_sum | solution.py:57
  200.1 1.6 fusion.15
  201.7 24.4 %fusion.10 = bf16[4,24,4,8,128]{4,1,3,2,0:T(8,128)(2,1)S(1)} fusion(f32[4,4,128,8,24]{2,4,3,1,0:T(8,128)} %fusion.15, f32[4,4,4096,24,8]{2,3,4,1,0:T(8,128)} %get-tuple-element.50, f32[4,4,8,24]{3,2,1,0:T(8,128)S(1)} %add.91, f32[4,4,8,24]{3,2,1,0:T(8,128)S(1)} %max.16, pred[4,4096]{1,0:T(4,128)(4,1)S(1)} %iota_compare_fusion, ...), kind=kOutput, calls=%fused_computation.33 | convolution fusion | flops 3284926464 | bytes 69509120 | tf_op jit(solution)/shard_map/skgqc,sckd->sqkgd/dot_general | solution.py:62
  226.3 0.3 reshape.312
  226.8 0.8 scatter_fusion
  227.6 0.8 and_reduce_fusion
  228.4 0.8 dynamic-slice_bitcast_fusion.2
  229.2 3.9 %collective-permute-start.5 = (bf16[24,4096]{1,0:T(8,128)(2,1)S(1)}, bf16[24,4096]{1,0:T(8,128)(2,1)S(1)}, u32[]{:S(2)}, u32[]{:S(2)}) collective-permute-start(bf16[24,4096]{1,0:T(8,128)(2,1)S(1)} %copy-done.6), channel_id=1, source_target_pairs={{2,0},{4,2},{6,4},{8,6},{10,8},{12,10},{14,12},{16,14},{18,16},{20... | collective-permute-start | bytes 589832 | tf_op jit(solution)/shard_map/ppermute | solution.py:16
  233.2 1.4 pad_add_fusion.4
  234.6 4.8 %collective-permute-done.6 = bf16[24,1024]{1,0:T(8,128)(2,1)S(1)} collective-permute-done((bf16[24,1024]{1,0:T(8,128)(2,1)S(1)}, bf16[24,1024]{1,0:T(8,128)(2,1)S(1)}, u32[]{:S(2)}, u32[]{:S(2)}) %collective-permute-start.6) | collective-permute-done | bytes 49184 | tf_op jit(solution)/shard_map/ppermute | solution.py:16
  239.4 1.7 collective-permute-done.7
  241.2 1.0 copy.44
  242.4 1.7 fusion.35
  244.0 1.9 stack.27
  245.9 1.9 stack.28
  248.1 0.7 copy-done.4
  248.8 0.9 bitcast_reduce_fusion.1
  250.0 1.0 fusion.5
  251.0 0.3 fusion.19
  251.4 1.1 fusion.13
  252.8 0.6 select_dynamic-update-slice_fusion.1
  253.4 0.7 select_dynamic-update-slice_fusion
  254.2 17.4 %fusion.36 = f32[144,4096]{1,0:T(8,128)} fusion(bf16[144,4096]{1,0:T(8,128)(2,1)S(1)} %bitcast.145, bf16[4096,4096]{1,0:T(8,128)(2,1)} %all-gather.2.cloned.1.call-done), kind=kOutput, calls=%fused_computation.100 | convolution fusion | flops 4831838208 | bytes 37093376 | tf_op jit(solution)/shard_map/dot_general | solution.py:101
  271.6 36.4 %reduce-scatter.2.cloned.1.call-done = f32[144,2048]{1,0:T(8,128)} async-done(((f32[144,4096]{1,0:T(8,128)}), f32[144,2048]{1,0:T(8,128)}) %reduce-scatter.2.cloned.1.call-update) | async-done | bytes 1179664 | tf_op jit(solution)/shard_map/reduce_scatter | solution.py:107
  307.9 2.2 convert_element_type.36
  (73 shorter events, 2.2 us)
Async XLA Ops:
  6.5 34.5 %copy-start = (s32[6]{0:T(128)S(1)}, s32[6]{0:T(128)}, u32[]{:S(2)}) copy-start(s32[6]{0:T(128)} %param.14) | copy-start | bytes 76
  6.5 31.0 %copy-start.2 = (bf16[6,24,4096]{2,1,0:T(8,128)(2,1)S(1)}, bf16[6,24,4096]{2,1,0:T(8,128)(2,1)}, u32[]{:S(2)}) copy-start(bf16[6,24,4096]{2,1,0:T(8,128)(2,1)} %param.11) | copy-start | bytes 3538948
  6.5 247.6 %all-gather.2.cloned.1.call-start = ((), (), s32[]{:S(2)}) async-start(), calls=%async_computation.1 | async-start | bytes 35651584 | tf_op jit(solution)/shard_map/all_gather | solution.py:103
  7.3 34.4 %copy-start.7 = (s32[6,32]{1,0:T(8,128)S(1)}, s32[6,32]{1,0:T(8,128)}, u32[]{:S(2)}) copy-start(s32[6,32]{1,0:T(8,128)} %param.15) | copy-start | bytes 2308
  7.3 300.6 %reduce-scatter.2.cloned.1.call-start = ((), (), s32[]{:S(2)}) async-start(), calls=%async_computation.2 | async-start | bytes 3538944 | tf_op jit(solution)/shard_map/reduce_scatter | solution.py:107
  13.8 215.4 %collective-permute-start.2 = (s32[1]{0:T(128)}, s32[1]{0:T(128)}, u32[]{:S(2)}, u32[]{:S(2)}) collective-permute-start(s32[1]{0:T(128)} %get-tuple-element.45), channel_id=1, source_target_pairs={{30,0},{0,2},{2,4},{4,6},{6,8},{8,10},{10,12},{12,14},{14,16},{16,... | collective-permute-start | bytes 20 | tf_op jit(solution)/shard_map/ppermute | solution.py:16
  14.2 218.9 %collective-permute-start.3 = (s32[1]{0:T(128)}, s32[1]{0:T(128)}, u32[]{:S(2)}, u32[]{:S(2)}) collective-permute-start(s32[1]{0:T(128)} %get-tuple-element.46), channel_id=1, source_target_pairs={{2,0},{4,2},{6,4},{8,6},{10,8},{12,10},{14,12},{16,14},{18,16},{20... | collective-permute-start | bytes 20 | tf_op jit(solution)/shard_map/ppermute | solution.py:16
  26.5 217.5 %collective-permute-start = (bf16[4,128,1024]{2,1,0:T(8,128)(2,1)}, bf16[4,128,1024]{2,1,0:T(8,128)(2,1)}, u32[]{:S(2)}, u32[]{:S(2)}) collective-permute-start(bf16[4,128,1024]{2,1,0:T(8,128)(2,1)} %gather_fusion.5), channel_id=1, source_target_pairs={{30,0},{0,2},{2,4},{4,6},{6,8},{8,10},{10,12},{12,14},{14,16},{16,... | collective-permute-start | bytes 3145736 | tf_op jit(solution)/shard_map/ppermute | solution.py:16
  33.3 212.6 %collective-permute-start.1 = (bf16[4,128,1024]{2,1,0:T(8,128)(2,1)}, bf16[4,128,1024]{2,1,0:T(8,128)(2,1)}, u32[]{:S(2)}, u32[]{:S(2)}) collective-permute-start(bf16[4,128,1024]{2,1,0:T(8,128)(2,1)} %gather_fusion.6), channel_id=1, source_target_pairs={{2,0},{4,2},{6,4},{8,6},{10,8},{12,10},{14,12},{16,14},{18,16},{20... | collective-permute-start | bytes 3145736 | tf_op jit(solution)/shard_map/ppermute | solution.py:16
  38.3 202.9 %collective-permute-start.4 = (bf16[24,4096]{1,0:T(8,128)(2,1)}, bf16[24,4096]{1,0:T(8,128)(2,1)}, u32[]{:S(2)}, u32[]{:S(2)}) collective-permute-start(bf16[24,4096]{1,0:T(8,128)(2,1)} %get-tuple-element.36), channel_id=1, source_target_pairs={{30,0},{0,2},{2,4},{4,6},{6,8},{8,10},{10,12},{12,14},{14,16},{16,... | collective-permute-start | bytes 589832 | tf_op jit(solution)/shard_map/ppermute | solution.py:16
  40.5 0.6 copy-start.10
  60.9 55.2 %copy-start.5 = (bf16[6,24,1024]{2,1,0:T(8,128)(2,1)S(1)}, bf16[6,24,1024]{2,1,0:T(8,128)(2,1)}, u32[]{:S(2)}) copy-start(bf16[6,24,1024]{2,1,0:T(8,128)(2,1)} %param.12) | copy-start | bytes 884740
  116.7 1.5 copy-start.8
  226.2 0.7 copy-start.11
  226.2 1.4 copy-start.12
  226.2 3.0 copy-start.6
  226.7 15.7 %copy-start.9 = (pred[24,24]{0,1:T(8,128)(4,1)S(1)}, pred[24,24]{0,1:T(8,128)(4,1)}, u32[]{:S(2)}) copy-start(pred[24,24]{0,1:T(8,128)(4,1)} %copy-done.8) | copy-start | bytes 1732
  229.2 12.9 %collective-permute-start.5 = (bf16[24,4096]{1,0:T(8,128)(2,1)S(1)}, bf16[24,4096]{1,0:T(8,128)(2,1)S(1)}, u32[]{:S(2)}, u32[]{:S(2)}) collective-permute-start(bf16[24,4096]{1,0:T(8,128)(2,1)S(1)} %copy-done.6), channel_id=1, source_target_pairs={{2,0},{4,2},{6,4},{8,6},{10,8},{12,10},{14,12},{16,14},{18,16},{20... | collective-permute-start | bytes 589832 | tf_op jit(solution)/shard_map/ppermute | solution.py:16
  233.2 6.2 %collective-permute-start.6 = (bf16[24,1024]{1,0:T(8,128)(2,1)S(1)}, bf16[24,1024]{1,0:T(8,128)(2,1)S(1)}, u32[]{:S(2)}, u32[]{:S(2)}) collective-permute-start(bf16[24,1024]{1,0:T(8,128)(2,1)S(1)} %get-tuple-element.40), channel_id=1, source_target_pairs={{30,0},{0,2},{2,4},{4,6},{6,8},{8,10},{10,12},{12,14},{14,16},{16,... | collective-permute-start | bytes 147464 | tf_op jit(solution)/shard_map/ppermute | solution.py:16
  239.4 1.8 collective-permute-start.7
  242.4 1.7 copy-start.3
  247.8 1.0 copy-start.4
  247.9 1.8 copy-start.1
Sparse Core Ops, SparseCore 0:
  9.0 194.9 all-gather.1
  271.7 36.1 reduce-scatter.1
where the time goes:
time: 319 us; the launch traced here: 317 us
  local copies, waits for them, and re-layouts  125 us (39%)
  matrix products  84.5 us (26%)
  waiting for transfers between devices  43.6 us (14%)
  other arithmetic  32.4 us (10%)
  between operations  17.6 us (6%)
  starting transfers between devices  13.6 us (4%)
    reshape x1, local copies, waits for them, and re-layouts, attend(): cache_block = page_list.reshape(slots, cached_rows, kv_heads, 2 * head_dim)  55 us
    dot_general x2, matrix products, attend(): jnp.einsum('sqkgd,sckd->skgqc', query_head_rows, cache_keys, preferred_el...  36.5 us
    reduce_scatter x1, waiting for transfers between devices, per_device(): lax.psum_scatter(partial_sum, 'tp', scatter_dimension=1, tiled=True)  36.4 us
    dot_general x2, matrix products, attend(): jnp.einsum('skgqc,sckd->sqkgd', cache_weights, cache_values, preferred_el...  25.5 us
    slice x1, local copies, waits for them, and re-layouts, attend(): cache_values = cache_block[..., head_dim:]  23.8 us
    reduce_sum x2, other arithmetic, attend(): jnp.sum(cache_powers, axis=-1, keepdims=True)  22.9 us
    gather x1, local copies, waits for them, and re-layouts, per_device(): key_value_pages[page_table[stayers]]  17.9 us
    dot_general x1, matrix products, per_device(): lax.dot_general(flat, lax.all_gather(w_out, 'req', axis=0, tiled=True), (...  17.4 us
  transfers between devices with their start and end apart: 10, of which 3 were waited for; matrix products, arithmetic and copies ran while one was open for 70% of the time, Pallas kernels for 0%

commit v1 on v0

v1 whole, which is shorter than its diff:
```python
import functools

import jax
import jax.numpy as jnp
from jax import lax
from jax.experimental import pallas as pl
from jax.experimental.pallas import tpu as pltpu
from jax.sharding import PartitionSpec as P

HEAD_SIZE = 128
PAGE_GROUP = 4
LOG2E = 1.4426950408889634
MASKED = -1e30


def passed_along(block, axis, distance):
    devices = range(lax.axis_size(axis))
    route = [((i - distance) % len(devices), i) for i in devices]
    return lax.ppermute(block, axis, route)


def nt(a, b):
    return lax.dot_general(a, b, (((1,), (1,)), ((), ())), preferred_element_type=jnp.float32)


def attend_kernel(kv_heads, group, len_ref, tab_ref, q_ref, f_ref, pages_ref, o_ref, qs, ms, ls, acc):
    slot = pl.program_id(0)
    tokens = q_ref.shape[1]
    page = pages_ref.shape[1]
    rows = group * tokens
    maxp = tab_ref.shape[1]
    length = len_ref[slot]
    factor = HEAD_SIZE ** (-0.5) * LOG2E
    span = PAGE_GROUP * page
    groups = (length + span - 1) // span
    token = lax.broadcasted_iota(jnp.int32, (rows, tokens), 0) % tokens
    newer = lax.broadcasted_iota(jnp.int32, (rows, tokens), 1)
    for g in range(kv_heads):
        heads = [
            q_ref[0, :, (g * group + h) * HEAD_SIZE : (g * group + h + 1) * HEAD_SIZE].astype(jnp.float32)
            for h in range(group)
        ]
        q = jnp.concatenate(heads, axis=0).astype(jnp.bfloat16)
        qs[g] = q
        key = f_ref[0, :, 2 * g * HEAD_SIZE : (2 * g + 1) * HEAD_SIZE]
        value = f_ref[0, :, (2 * g + 1) * HEAD_SIZE : (2 * g + 2) * HEAD_SIZE]
        s = jnp.where(newer <= token, nt(q, key), MASKED)
        m = jnp.max(s, axis=-1, keepdims=True)
        p = jnp.exp2((s - m) * factor)
        ms[g] = m
        ls[g] = jnp.sum(p, axis=-1, keepdims=True)
        acc[g] = jnp.dot(p.astype(jnp.bfloat16), value, preferred_element_type=jnp.float32)

    def body(at, carry):
        ids = [tab_ref[slot, jnp.minimum(at * PAGE_GROUP + u, maxp - 1)] for u in range(PAGE_GROUP)]
        pos = at * span + lax.broadcasted_iota(jnp.int32, (rows, span), 1)
        valid = pos < length
        for g in range(kv_heads):
            keys = jnp.concatenate(
                [pages_ref[i, :, 2 * g * HEAD_SIZE : (2 * g + 1) * HEAD_SIZE] for i in ids], axis=0
            )
            values = jnp.concatenate(
                [pages_ref[i, :, (2 * g + 1) * HEAD_SIZE : (2 * g + 2) * HEAD_SIZE] for i in ids], axis=0
            )
            s = jnp.where(valid, nt(qs[g], keys), MASKED)
            before = ms[g]
            m = jnp.maximum(before, jnp.max(s, axis=-1, keepdims=True))
            fade = jnp.exp2((before - m) * factor)
            p = jnp.exp2((s - m) * factor)
            ms[g] = m
            ls[g] = ls[g] * fade + jnp.sum(p, axis=-1, keepdims=True)
            acc[g] = acc[g] * fade + jnp.dot(
                p.astype(jnp.bfloat16), values, preferred_element_type=jnp.float32
            )
        return carry

    lax.fori_loop(0, groups, body, 0)
    for g in range(kv_heads):
        o = acc[g] / ls[g]
        for h in range(group):
            o_ref[0, :, (g * group + h) * HEAD_SIZE : (g * group + h + 1) * HEAD_SIZE] = o[
                h * tokens : (h + 1) * tokens
            ].astype(jnp.bfloat16)


def attend(queries, fresh_kv, pages, lengths, table):
    slots, tokens, width = queries.shape
    kv_heads = fresh_kv.shape[2] // (2 * HEAD_SIZE)
    group = width // (kv_heads * HEAD_SIZE)
    rows = group * tokens
    return pl.pallas_call(
        functools.partial(attend_kernel, kv_heads, group),
        out_shape=jax.ShapeDtypeStruct(queries.shape, jnp.bfloat16),
        grid_spec=pltpu.PrefetchScalarGridSpec(
            num_scalar_prefetch=2,
            grid=(slots,),
            in_specs=[
                pl.BlockSpec((1, tokens, width), lambda s, a, b: (s, 0, 0)),
                pl.BlockSpec((1, tokens, fresh_kv.shape[2]), lambda s, a, b: (s, 0, 0)),
                pl.BlockSpec(pages.shape, lambda s, a, b: (0, 0, 0), pipeline_mode=pl.Buffered(1)),
            ],
            out_specs=pl.BlockSpec((1, tokens, width), lambda s, a, b: (s, 0, 0)),
            scratch_shapes=[
                pltpu.VMEM((kv_heads, rows, HEAD_SIZE), jnp.bfloat16),
                pltpu.VMEM((kv_heads, rows, 1), jnp.float32),
                pltpu.VMEM((kv_heads, rows, 1), jnp.float32),
                pltpu.VMEM((kv_heads, rows, HEAD_SIZE), jnp.float32),
            ],
        ),
        compiler_params=pltpu.CompilerParams(vmem_limit_bytes=40 << 20),
        cost_estimate=pl.CostEstimate(
            flops=4 * rows * kv_heads * pages.shape[0] * pages.shape[1] * HEAD_SIZE,
            transcendentals=rows * kv_heads * pages.shape[0] * pages.shape[1],
            bytes_accessed=pages.size * 2 + queries.size * 4,
        ),
    )(lengths, table, queries, fresh_kv, pages)


def per_device(queries, fresh_kv, key_value_pages, cache_lengths, page_table, movers, w_out):
    slots, tokens, width = queries.shape
    to_next = movers[0, 0]
    to_prev = movers[0, 1]
    attended = attend(queries, fresh_kv, key_value_pages, cache_lengths, page_table)
    from_left = passed_along(attended[to_next], "req", 1)
    from_right = passed_along(attended[to_prev], "req", -1)
    slot_ids = jnp.arange(slots, dtype=jnp.int32)[:, None, None]
    placed = jnp.where(
        slot_ids == to_next, from_left[None], jnp.where(slot_ids == to_prev, from_right[None], attended)
    )
    flat = placed.reshape(slots * tokens, width)
    partial_sum = lax.dot_general(
        flat,
        lax.all_gather(w_out, "req", axis=0, tiled=True),
        (((1,), (1,)), ((), ())),
        preferred_element_type=jnp.float32,
    )
    return lax.psum_scatter(partial_sum, "tp", scatter_dimension=1, tiled=True).astype(jnp.bfloat16)


def solution(mesh):
    return jax.shard_map(
        per_device,
        mesh=mesh,
        in_specs=(
            P("req", None, "tp"),
            P("req", None, "tp"),
            P("req", None, "tp"),
            P("req"),
            P("req", None),
            P("req", None),
            P("req", "tp"),
        ),
        out_specs=P("req", "tp"),
        check_vma=False,
    )
```

time: 319 us -> 245 us (0.77)
  waiting for transfers between devices: 43.6 us -> 169 us
  local copies, waits for them, and re-layouts: 125 us -> 0.65 us
  matrix products: 84.5 us -> 17.3 us
  other arithmetic: 32.4 us -> 3.66 us
  Pallas kernels: 0 us -> 22.8 us
    all_gather x1, waiting for transfers between devices: 0.02 us -> 127 us  [per_device(): lax.all_gather(w_out, 'req', axis=0, tiled=True)]
    dot_general x8 -> x0, matrix products: 67.2 us -> none  [the longest x2 36.5 us: attend(): jnp.einsum('sqkgd,sckd->skgqc', query_head_rows, cache_keys, preferred_el...]
    reshape x3 -> x0, local copies, waits for them, and re-layouts: 55.5 us -> none  [the longest x1 55 us: attend(): cache_block = page_list.reshape(slots, cached_rows, kv_heads, 2 * head_dim)]
    gather x7 -> x0, local copies, waits for them, and re-layouts: 33.6 us -> none  [the longest x1 17.9 us: per_device(): key_value_pages[page_table[stayers]]]
    slice x5 -> x0, local copies, waits for them, and re-layouts: 23.9 us -> none  [the longest x1 23.8 us: attend(): cache_values = cache_block[..., head_dim:]]
    reduce_sum x4 -> x0, other arithmetic: 23.5 us -> none  [the longest x2 22.9 us: attend(): jnp.sum(cache_powers, axis=-1, keepdims=True)]
    pallas_call x0 -> x1, Pallas kernels: none -> 22.8 us  [attend(): pl.pallas_call(functools.partial(attend_kernel, kv_heads, group), out_sha...]
    another operation x9 -> x0, local copies, waits for them, and re-layouts: 4.18 us -> none  [the longest x3 3.85 us: per_device(): jnp.stack([from_left[0], from_right[0]])]
  transfers between devices with their start and end apart: 10 -> 4, of which waited for: 3 -> 3; matrix products, arithmetic and copies ran while one was open for 70% -> 1% of each run, Pallas kernels for 0% -> 9%
where the time goes in v1:
time: 245 us
  waiting for transfers between devices  169 us (69%)
  Pallas kernels  22.8 us (9%)
  matrix products  17.3 us (7%)
  between operations  17.3 us (7%)
  starting transfers between devices  14.5 us (6%)
  other arithmetic  3.66 us (1%)
    all_gather x1, waiting for transfers between devices, per_device(): lax.all_gather(w_out, 'req', axis=0, tiled=True)  127 us
    reduce_scatter x1, waiting for transfers between devices, per_device(): lax.psum_scatter(partial_sum, 'tp', scatter_dimension=1, tiled=True)  35.2 us
    pallas_call x1, Pallas kernels, attend(): pl.pallas_call(functools.partial(attend_kernel, kv_heads, group), out_sha...  22.8 us
    dot_general x1, matrix products, per_device(): lax.dot_general(flat, lax.all_gather(w_out, 'req', axis=0, tiled=True), (...  17.3 us
    ppermute x2, starting transfers between devices, passed_along(): return lax.ppermute(block, axis, route)  14.4 us
    ppermute x2, waiting for transfers between devices, passed_along(): return lax.ppermute(block, axis, route)  6.2 us
  transfers between devices with their start and end apart: 4, of which 3 were waited for; matrix products, arithmetic and copies ran while one was open for 1% of the time, Pallas kernels for 9%

profile of v1, /device:TPU:0, one launch (start us, length us, event | category | flops | bytes accessed | tf_op | source)
XLA Modules:
  0.0 245.2 jit_solution(13432063646862592188)
XLA Ops:
  6.5 0.0 copy-start.4
  6.5 0.0 copy-start.2
  6.5 0.0 copy-start.3
  6.5 0.0 copy-start.1
  6.5 0.0 copy-start
  6.5 0.0 all-gather.2.cloned.1.call-start
  6.6 0.7 all-gather.2.cloned.1.call-update
  7.3 0.0 reduce-scatter.2.cloned.1.call-start
  7.3 0.0 copy-done.4
  7.3 0.6 fusion
  11.7 0.0 copy-done.2
  11.7 0.0 copy-done.3
  11.8 0.0 copy-done.1
  11.8 0.0 copy-done
  11.8 22.8 %shard_map.73 = bf16[6,24,4096]{2,1,0:T(8,128)(2,1)S(1)} custom-call(s32[6]{0:T(128)S(1)} %copy-done.3, s32[6,32]{1,0:T(8,128)S(1)} %copy-done.2, bf16[6,24,4096]{2,1,0:T(8,128)(2,1)S(1)} %copy-done, bf16[6,24,1024]{2,1,0:T(8,128)(2,1)S(1)} %copy-done.1, bf16[52,128,1024]{2,1,0:T(8,128)(2,1)} %pages_ref.1), custom_call_target="tpu_custom_call" | custom-call | flops 2617245696 | bytes 15990784 | tf_op jit(solution)/shard_map/pallas_call | solution.py:91
  34.7 4.0 %collective-permute-start = (bf16[24,4096]{1,0:T(8,128)(2,1)S(1)}, bf16[24,4096]{1,0:T(8,128)(2,1)S(1)}, u32[]{:S(2)}, u32[]{:S(2)}) collective-permute-start(bf16[24,4096]{1,0:T(8,128)(2,1)S(1)} %get-tuple-element.5), channel_id=1, source_target_pairs={{30,0},{0,2},{2,4},{4,6},{6,8},{8,10},{10,12},{12,14},{14,16},{16,... | collective-permute-start | bytes 589832 | tf_op jit(solution)/shard_map/ppermute | solution.py:19
  38.7 10.4 %collective-permute-start.1 = (bf16[24,4096]{1,0:T(8,128)(2,1)S(1)}, bf16[24,4096]{1,0:T(8,128)(2,1)S(1)}, u32[]{:S(2)}, u32[]{:S(2)}) collective-permute-start(bf16[24,4096]{1,0:T(8,128)(2,1)S(1)} %get-tuple-element.6), channel_id=1, source_target_pairs={{2,0},{4,2},{6,4},{8,6},{10,8},{12,10},{14,12},{16,14},{18,16},{20... | collective-permute-start | bytes 589832 | tf_op jit(solution)/shard_map/ppermute | solution.py:19
  49.1 1.3 iota_compare_fusion
  50.4 6.2 %collective-permute-done = bf16[24,4096]{1,0:T(8,128)(2,1)S(1)} collective-permute-done((bf16[24,4096]{1,0:T(8,128)(2,1)S(1)}, bf16[24,4096]{1,0:T(8,128)(2,1)S(1)}, u32[]{:S(2)}, u32[]{:S(2)}) %collective-permute-start) | collective-permute-done | bytes 196640 | tf_op jit(solution)/shard_map/ppermute | solution.py:19
  56.6 0.0 collective-permute-done.1
  56.6 0.2 select_select_fusion
  56.8 126.9 %all-gather.2.cloned.1.call-done = bf16[4096,4096]{1,0:T(8,128)(2,1)} async-done(((bf16[256,4096]{1,0:T(8,128)(2,1)}), bf16[4096,4096]{1,0:T(8,128)(2,1)}) %all-gather.2.cloned.1.call-update) | async-done | bytes 33554448 | tf_op jit(solution)/shard_map/all_gather | solution.py:133
  183.6 17.3 %fusion.1 = f32[144,4096]{1,0:T(8,128)} fusion(bf16[144,4096]{1,0:T(8,128)(2,1)S(1)} %bitcast.9, bf16[4096,4096]{1,0:T(8,128)(2,1)} %all-gather.2.cloned.1.call-done), kind=kOutput, calls=%fused_computation.6 | convolution fusion | flops 4831838208 | bytes 37093376 | tf_op jit(solution)/shard_map/dot_general | solution.py:131
  201.0 0.0 reduce-scatter.2.cloned.1.call-update
  201.0 35.2 %reduce-scatter.2.cloned.1.call-done = f32[144,2048]{1,0:T(8,128)} async-done(((f32[144,4096]{1,0:T(8,128)}), f32[144,2048]{1,0:T(8,128)}) %reduce-scatter.2.cloned.1.call-update) | async-done | bytes 1179664 | tf_op jit(solution)/shard_map/reduce_scatter | solution.py:137
  236.2 2.2 convert_element_type.3
  (1 shorter events, 0.0 us)
Async XLA Ops:
  6.5 0.8 copy-start.4
  6.5 5.2 %copy-start.2 = (s32[6,32]{1,0:T(8,128)S(1)}, s32[6,32]{1,0:T(8,128)}, u32[]{:S(2)}) copy-start(s32[6,32]{1,0:T(8,128)} %tab_ref.1) | copy-start | bytes 2308
  6.5 5.2 %copy-start.3 = (s32[6]{0:T(128)S(1)}, s32[6]{0:T(128)}, u32[]{:S(2)}) copy-start(s32[6]{0:T(128)} %len_ref.1) | copy-start | bytes 76
  6.5 5.2 %copy-start.1 = (bf16[6,24,1024]{2,1,0:T(8,128)(2,1)S(1)}, bf16[6,24,1024]{2,1,0:T(8,128)(2,1)}, u32[]{:S(2)}) copy-start(bf16[6,24,1024]{2,1,0:T(8,128)(2,1)} %f_ref.1) | copy-start | bytes 884740
  6.5 5.2 %copy-start = (bf16[6,24,4096]{2,1,0:T(8,128)(2,1)S(1)}, bf16[6,24,4096]{2,1,0:T(8,128)(2,1)}, u32[]{:S(2)}) copy-start(bf16[6,24,4096]{2,1,0:T(8,128)(2,1)} %q_ref.1) | copy-start | bytes 3538948
  6.5 177.1 %all-gather.2.cloned.1.call-start = ((), (), s32[]{:S(2)}) async-start(), calls=%async_computation.1 | async-start | bytes 35651584 | tf_op jit(solution)/shard_map/all_gather | solution.py:133
  7.3 228.9 %reduce-scatter.2.cloned.1.call-start = ((), (), s32[]{:S(2)}) async-start(), calls=%async_computation.2 | async-start | bytes 3538944 | tf_op jit(solution)/shard_map/reduce_scatter | solution.py:137
  34.7 21.9 %collective-permute-start = (bf16[24,4096]{1,0:T(8,128)(2,1)S(1)}, bf16[24,4096]{1,0:T(8,128)(2,1)S(1)}, u32[]{:S(2)}, u32[]{:S(2)}) collective-permute-start(bf16[24,4096]{1,0:T(8,128)(2,1)S(1)} %get-tuple-element.5), channel_id=1, source_target_pairs={{30,0},{0,2},{2,4},{4,6},{6,8},{8,10},{10,12},{12,14},{14,16},{16,... | collective-permute-start | bytes 589832 | tf_op jit(solution)/shard_map/ppermute | solution.py:19
  38.7 17.9 %collective-permute-start.1 = (bf16[24,4096]{1,0:T(8,128)(2,1)S(1)}, bf16[24,4096]{1,0:T(8,128)(2,1)S(1)}, u32[]{:S(2)}, u32[]{:S(2)}) collective-permute-start(bf16[24,4096]{1,0:T(8,128)(2,1)S(1)} %get-tuple-element.6), channel_id=1, source_target_pairs={{2,0},{4,2},{6,4},{8,6},{10,8},{12,10},{14,12},{16,14},{18,16},{20... | collective-permute-start | bytes 589832 | tf_op jit(solution)/shard_map/ppermute | solution.py:19
Sparse Core Ops, SparseCore 0:
  9.0 174.6 all-gather.1
  201.1 35.0 reduce-scatter.1

commit v2 on v1

--- a/solution.py
+++ b/solution.py
@@ -115,6 +115,234 @@
         ),
     )(lengths, table, queries, fresh_kv, pages)
 
+CHUNKS = 4
+MESH = pl.DeviceIdType.MESH
+
+
+def project_kernel(
+    n, a_ref, w_ref, o_ref, buf, part, theirs, summed, out,
+    ring_send, ring_recv, twin_send, twin_recv, x_send, x_recv, o_send, o_recv,
+):
+    me, t = lax.axis_index("req"), lax.axis_index("tp")
+    other = 1 - t
+    chips, cols = n // 2, n // 2
+    half = chips // 2
+    core, chip = me % 2, me // 2
+    twin = me + 1 - 2 * core
+    z, y = chip // 2, chip % 2
+    at = z + y * (chips - 1 - 2 * z)
+    wide = w_ref.shape[0]
+    depth = w_ref.shape[1] // CHUNKS
+
+    def owner(place, which):
+        place = (place + 2 * chips) % chips
+        far = place // half
+        return 2 * (2 * (place + far * (chips - 1 - 2 * place)) + far) + which
+
+    def place_of(step, side):
+        return at - step * (1 - 2 * side)
+
+    my_index = me * 2 + t
+
+    barrier = pltpu.get_barrier_semaphore()
+
+    def greet(i, carry):
+        target = (my_index + i) % (2 * n)
+        pl.semaphore_signal(
+            barrier, inc=1, device_id={"req": target // 2, "tp": target % 2}, device_id_type=MESH
+        )
+        return carry
+
+    lax.fori_loop(1, 2 * n, greet, 0)
+    buf[me] = a_ref[...]
+    pl.semaphore_wait(barrier, 2 * n - 1)
+
+    def ring_copy(step, side, c):
+        where = buf.at[owner(place_of(step, side), core), side, :, pl.ds(c * depth, depth)]
+        return pltpu.make_async_remote_copy(
+            src_ref=where, dst_ref=where,
+            send_sem=ring_send.at[step, side, c], recv_sem=ring_recv.at[step, side, c],
+            device_id={"req": owner(at + 1 - 2 * side, core), "tp": t}, device_id_type=MESH,
+        )
+
+    def ring_arrival(step, side, c):
+        where = buf.at[owner(place_of(step + 1, side), core), side, :, pl.ds(c * depth, depth)]
+        return pltpu.make_async_remote_copy(
+            src_ref=where, dst_ref=where,
+            send_sem=ring_send.at[step, side, c], recv_sem=ring_recv.at[step, side, c],
+            device_id={"req": owner(at + 1 - 2 * side, core), "tp": t}, device_id_type=MESH,
+        )
+
+    def twin_copy(step, side, which):
+        where = buf.at[owner(place_of(step, side), which), side]
+        return pltpu.make_async_remote_copy(
+            src_ref=where, dst_ref=where,
+            send_sem=twin_send.at[step, side], recv_sem=twin_recv.at[step, side],
+            device_id={"req": twin, "tp": t}, device_id_type=MESH,
+        )
+
+    def x_copy(o):
+        return pltpu.make_async_remote_copy(
+            src_ref=part.at[o, other], dst_ref=theirs.at[o],
+            send_sem=x_send.at[o], recv_sem=x_recv.at[o],
+            device_id={"req": me, "tp": other}, device_id_type=MESH,
+        )
+
+    dest_tp, dest_col = me // cols, me % cols
+
+    def out_copy(o):
+        return pltpu.make_async_remote_copy(
+            src_ref=summed.at[o],
+            dst_ref=out.at[t, :, pl.ds(pl.multiple_of(dest_col * wide, wide), wide)],
+            send_sem=o_send.at[o], recv_sem=o_recv.at[t, dest_col],
+            device_id={"req": o, "tp": dest_tp}, device_id_type=MESH,
+        )
+
+    def multiply(o, side):
+        part[o, side] = nt(buf[o, side], w_ref[...])
+
+    def reduce(o):
+        x_copy(o).wait_recv()
+        summed[o] = (part[o, t] + theirs[o]).astype(jnp.bfloat16)
+
+    for c in range(CHUNKS):
+        for side in range(2):
+            ring_copy(0, side, c).start()
+    for side in range(2):
+        twin_copy(0, side, core).start()
+    for side in range(2):
+        multiply(me, side)
+    x_copy(me).start()
+
+    def step_body(step, carry):
+        for c in range(CHUNKS):
+            for side in range(2):
+                ring_arrival(step - 1, side, c).wait_recv()
+
+                @pl.when(step < chips - 1)
+                def _():
+                    ring_copy(step, side, c).start()
+
+        for side in range(2):
+            twin_copy(step, side, core).start()
+        for side in range(2):
+            multiply(owner(place_of(step, side), core), side)
+        x_copy(owner(place_of(step, other), core)).start()
+        for side in range(2):
+            twin_copy(step - 1, side, 1 - core).wait_recv()
+            multiply(owner(place_of(step - 1, side), 1 - core), side)
+        x_copy(owner(place_of(step - 1, other), 1 - core)).start()
+
+        @pl.when(step >= 2)
+        def _():
+            mine = owner(place_of(step - 1, t), core)
+            reduce(mine)
+            out_copy(mine).start()
+            twins = owner(place_of(step - 2, t), 1 - core)
+            reduce(twins)
+            out_copy(twins).start()
+
+        return carry
+
+    lax.fori_loop(1, chips, step_body, 0)
+
+    for side in range(2):
+        twin_copy(chips - 1, side, 1 - core).wait_recv()
+        multiply(owner(place_of(chips - 1, side), 1 - core), side)
+    x_copy(owner(place_of(chips - 1, other), 1 - core)).start()
+
+    reduce(me)
+
+    @pl.when(dest_tp == t)
+    def _():
+        out[t, :, pl.ds(pl.multiple_of(dest_col * wide, wide), wide)] = summed[me]
+
+    @pl.when(dest_tp != t)
+    def _():
+        out_copy(me).start()
+
+    for o in (
+        owner(place_of(chips - 1, t), core),
+        owner(place_of(chips - 2, t), 1 - core),
+        owner(place_of(chips - 1, t), 1 - core),
+    ):
+        reduce(o)
+        out_copy(o).start()
+
+    def ring_done(step, carry):
+        for side in range(2):
+            for c in range(CHUNKS):
+                ring_copy(step, side, c).wait_send()
+        return carry
+
+    def twin_done(step, carry):
+        for side in range(2):
+            twin_copy(step, side, core).wait_send()
+        return carry
+
+    def x_done(o, carry):
+        x_copy(o).wait_send()
+
+        @pl.when(jnp.logical_or(o != me, dest_tp != t))
+        def _():
+            out_copy(o).wait_send()
+
+        return carry
+
+    lax.fori_loop(0, chips - 1, ring_done, 0)
+    lax.fori_loop(0, chips, twin_done, 0)
+    lax.fori_loop(0, n, x_done, 0)
+
+    def arrived(j, carry):
+        for h in range(2):
+            @pl.when(jnp.logical_or(t * cols + j != me, t != h))
+            def _():
+                where = out.at[h, :, pl.ds(pl.multiple_of(j * wide, wide), wide)]
+                pltpu.make_async_remote_copy(
+                    src_ref=summed.at[0], dst_ref=where,
+                    send_sem=o_send.at[0], recv_sem=o_recv.at[h, j],
+                    device_id={"req": twin, "tp": t}, device_id_type=MESH,
+                ).wait_recv()
+
+        return carry
+
+    lax.fori_loop(0, cols, arrived, 0)
+    o_ref[...] = out[...]
+
+
+def project(flat, w_out):
+    n = lax.axis_size("req")
+    rows, width = flat.shape
+    wide = w_out.shape[0]
+    side, cols = rows // 2, n // 2
+    dma = pltpu.SemaphoreType.DMA
+    vmem = pl.BlockSpec(memory_space=pltpu.VMEM)
+    done = pl.pallas_call(
+        functools.partial(project_kernel, n),
+        out_shape=jax.ShapeDtypeStruct((2, side, cols * wide), jnp.bfloat16),
+        in_specs=[vmem, vmem],
+        out_specs=vmem,
+        scratch_shapes=[
+            pltpu.VMEM((n, 2, side, width), jnp.bfloat16),
+            pltpu.VMEM((n, 2, side, wide), jnp.float32),
+            pltpu.VMEM((n, side, wide), jnp.float32),
+            pltpu.VMEM((n, side, wide), jnp.bfloat16),
+            pltpu.VMEM((2, side, cols * wide), jnp.bfloat16),
+            dma((cols - 1, 2, CHUNKS)),
+            dma((cols - 1, 2, CHUNKS)),
+            dma((cols, 2)),
+            dma((cols, 2)),
+            dma((n,)),
+            dma((n,)),
+            dma((n,)),
+            dma((2, cols)),
+        ],
+        compiler_params=pltpu.CompilerParams(
+            collective_id=0, has_side_effects=True, vmem_limit_bytes=48 << 20
+        ),
+    )(flat.reshape(2, side, width), w_out)
+    return done.reshape(rows, cols * wide)
+
 
 def per_device(queries, fresh_kv, key_value_pages, cache_lengths, page_table, movers, w_out):
     slots, tokens, width = queries.shape
@@ -128,6 +356,8 @@
         slot_ids == to_next, from_left[None], jnp.where(slot_ids == to_prev, from_right[None], attended)
     )
     flat = placed.reshape(slots * tokens, width)
+    if lax.axis_size("tp") == 2 and lax.axis_size("req") % 4 == 0:
+        return project(flat, w_out)
     partial_sum = lax.dot_general(
         flat,
         lax.all_gather(w_out, "req", axis=0, tiled=True),

time: 245 us -> 176 us (0.72); the launches traced: 245 us -> 173 us
  waiting for transfers between devices: 169 us -> 1.91 us
  Pallas kernels: 22.8 us -> 153 us
  matrix products: 17.3 us -> 0 us
  between operations: 17.3 us -> 3.87 us
  starting transfers between devices: 14.5 us -> 5.82 us
  local copies, waits for them, and re-layouts: 0.65 us -> 7.13 us
    all_gather x1 -> x0, waiting for transfers between devices: 127 us -> none  [per_device(): lax.all_gather(w_out, 'req', axis=0, tiled=True)]
    pallas_call x0 -> x1, Pallas kernels: none -> 125 us  [project(): pl.pallas_call(functools.partial(project_kernel, n), out_shape=jax.ShapeD...]
    reduce_scatter x1 -> x0, waiting for transfers between devices: 35.2 us -> none  [per_device(): lax.psum_scatter(partial_sum, 'tp', scatter_dimension=1, tiled=True)]
    dot_general x1 -> x0, matrix products: 17.3 us -> none  [per_device(): lax.dot_general(flat, lax.all_gather(w_out, 'req', axis=0, tiled=True), (...]
    ppermute x2, starting transfers between devices: 14.4 us -> 5.82 us  [passed_along(): return lax.ppermute(block, axis, route)]
    unnamed x10 -> x11, local copies, waits for them, and re-layouts: 0.02 us -> 5.74 us
    pallas_call x1, Pallas kernels: 22.8 us -> 28.1 us  [attend(): pl.pallas_call(functools.partial(attend_kernel, kv_heads, group), out_sha...]
    ppermute x2, waiting for transfers between devices: 6.2 us -> 1.91 us  [passed_along(): return lax.ppermute(block, axis, route)]
  transfers between devices with their start and end apart: 4 -> 2, of which waited for: 3 -> 2; matrix products, arithmetic and copies ran while one was open for 1% -> 1% of each run, Pallas kernels for 9% -> 0%
where the time goes in v2:
time: 176 us; the launch traced here: 173 us
  Pallas kernels  153 us (87%)
  local copies, waits for them, and re-layouts  7.13 us (4%)
  starting transfers between devices  5.82 us (3%)
  between operations  3.87 us (2%)
  waiting for transfers between devices  1.91 us (1%)
    pallas_call x1, Pallas kernels, project(): pl.pallas_call(functools.partial(project_kernel, n), out_shape=jax.ShapeD...  125 us
    pallas_call x1, Pallas kernels, attend(): pl.pallas_call(functools.partial(attend_kernel, kv_heads, group), out_sha...  28.1 us
    ppermute x2, starting transfers between devices, passed_along(): return lax.ppermute(block, axis, route)  5.82 us
    unnamed x11, local copies, waits for them, and re-layouts  5.74 us
  transfers between devices with their start and end apart: 2, of which 2 were waited for; matrix products, arithmetic and copies ran while one was open for 1% of the time, Pallas kernels for 0%

profile of v2, /device:TPU:0, one launch (start us, length us, event | category | flops | bytes accessed | tf_op | source)
XLA Modules:
  0.0 173.1 jit_solution(14337914995678811683)
XLA Ops:
  0.0 1.4 fusion
  5.2 0.0 copy-start.1
  5.2 1.3 copy-done.1
  6.5 0.0 copy-start.2
  6.5 1.0 copy-done.2
  7.4 0.0 copy-start.3
  7.4 0.7 copy-done.3
  8.1 0.0 copy-start.4
  8.1 0.7 copy-done.4
  8.8 28.1 %shard_map.73 = bf16[6,24,4096]{2,1,0:T(8,128)(2,1)S(1)} custom-call(s32[6]{0:T(128)S(1)} %copy-done.4, s32[6,32]{1,0:T(8,128)S(1)} %copy-done.3, bf16[6,24,4096]{2,1,0:T(8,128)(2,1)S(1)} %copy-done.1, bf16[6,24,1024]{2,1,0:T(8,128)(2,1)S(1)} %copy-done.2, bf16[52,128,1024]{2,1,0:T(8,128)(2,1)} %pages_ref.1), custom_call_target="tpu_custom_call" | custom-call | flops 2617245696 | bytes 15990784 | tf_op jit(solution)/shard_map/pallas_call | solution.py:91
  36.9 5.8 %collective-permute-start = (bf16[24,4096]{1,0:T(8,128)(2,1)S(1)}, bf16[24,4096]{1,0:T(8,128)(2,1)S(1)}, u32[]{:S(2)}, u32[]{:S(2)}) collective-permute-start(bf16[24,4096]{1,0:T(8,128)(2,1)S(1)} %get-tuple-element.5), channel_id=1, source_target_pairs={{30,0},{0,2},{2,4},{4,6},{6,8},{8,10},{10,12},{12,14},{14,16},{16,... | collective-permute-start | bytes 589832 | tf_op jit(solution)/shard_map/ppermute | solution.py:19
  42.8 0.0 collective-permute-start.1
  42.8 1.3 iota_compare_fusion
  44.1 0.7 collective-permute-done
  44.8 1.2 collective-permute-done.1
  46.0 0.0 copy-start
  46.0 0.2 select_select_fusion
  46.2 1.3 copy-done
  47.6 124.7 %shard_map.74 = bf16[2,72,2048]{2,1,0:T(8,128)(2,1)S(1)} custom-call(bf16[2,72,4096]{2,1,0:T(8,128)(2,1)S(1)} %bitcast.8, bf16[256,4096]{1,0:T(8,128)(2,1)S(1)} %copy-done), custom_call_target="tpu_custom_call" | custom-call | tf_op jit(solution)/shard_map/pallas_call | solution.py:320
  172.3 0.8 copy.9
  (1 shorter events, 0.0 us)
Async XLA Ops:
  5.2 1.3 copy-start.1
  6.5 1.0 copy-start.2
  7.4 0.7 copy-start.3
  8.1 0.7 copy-start.4
  36.9 7.8 %collective-permute-start = (bf16[24,4096]{1,0:T(8,128)(2,1)S(1)}, bf16[24,4096]{1,0:T(8,128)(2,1)S(1)}, u32[]{:S(2)}, u32[]{:S(2)}) collective-permute-start(bf16[24,4096]{1,0:T(8,128)(2,1)S(1)} %get-tuple-element.5), channel_id=1, source_target_pairs={{30,0},{0,2},{2,4},{4,6},{6,8},{8,10},{10,12},{12,14},{14,16},{16,... | collective-permute-start | bytes 589832 | tf_op jit(solution)/shard_map/ppermute | solution.py:19
  42.8 3.2 %collective-permute-start.1 = (bf16[24,4096]{1,0:T(8,128)(2,1)S(1)}, bf16[24,4096]{1,0:T(8,128)(2,1)S(1)}, u32[]{:S(2)}, u32[]{:S(2)}) collective-permute-start(bf16[24,4096]{1,0:T(8,128)(2,1)S(1)} %get-tuple-element.6), channel_id=1, source_target_pairs={{2,0},{4,2},{6,4},{8,6},{10,8},{12,10},{14,12},{16,14},{18,16},{20... | collective-permute-start | bytes 589832 | tf_op jit(solution)/shard_map/ppermute | solution.py:19
  46.0 1.6 copy-start

commit v3 on v2

--- a/solution.py
+++ b/solution.py
@@ -8,7 +8,7 @@
 from jax.sharding import PartitionSpec as P
 
 HEAD_SIZE = 128
-PAGE_GROUP = 4
+PAGE_GROUP = 8
 LOG2E = 1.4426950408889634
 MASKED = -1e30
 
@@ -55,14 +55,16 @@
         ids = [tab_ref[slot, jnp.minimum(at * PAGE_GROUP + u, maxp - 1)] for u in range(PAGE_GROUP)]
         pos = at * span + lax.broadcasted_iota(jnp.int32, (rows, span), 1)
         valid = pos < length
+        def side(g, which):
+            first = (2 * g + which) * HEAD_SIZE
+            return jnp.concatenate([pages_ref[i, :, first : first + HEAD_SIZE] for i in ids], axis=0)
+
+        def scored(g):
+            return jnp.where(valid, nt(qs[g], side(g, 0)), MASKED)
+
+        s = scored(0)
         for g in range(kv_heads):
-            keys = jnp.concatenate(
-                [pages_ref[i, :, 2 * g * HEAD_SIZE : (2 * g + 1) * HEAD_SIZE] for i in ids], axis=0
-            )
-            values = jnp.concatenate(
-                [pages_ref[i, :, (2 * g + 1) * HEAD_SIZE : (2 * g + 2) * HEAD_SIZE] for i in ids], axis=0
-            )
-            s = jnp.where(valid, nt(qs[g], keys), MASKED)
+            following = scored(g + 1) if g + 1 < kv_heads else None
             before = ms[g]
             m = jnp.maximum(before, jnp.max(s, axis=-1, keepdims=True))
             fade = jnp.exp2((before - m) * factor)
@@ -70,8 +72,9 @@
             ms[g] = m
             ls[g] = ls[g] * fade + jnp.sum(p, axis=-1, keepdims=True)
             acc[g] = acc[g] * fade + jnp.dot(
-                p.astype(jnp.bfloat16), values, preferred_element_type=jnp.float32
+                p.astype(jnp.bfloat16), side(g, 1), preferred_element_type=jnp.float32
             )
+            s = following
         return carry
 
     lax.fori_loop(0, groups, body, 0)

time: 176 us -> 169 us (0.960)
  Pallas kernels: 153 us -> 148 us
    pallas_call x1, Pallas kernels: 125 us -> 122 us  [project(): pl.pallas_call(functools.partial(project_kernel, n), out_shape=jax.ShapeD...]
    pallas_call x1, Pallas kernels: 28.1 us -> 26.2 us  [attend(): pl.pallas_call(functools.partial(attend_kernel, kv_heads, group), out_sha...]
  transfers between devices with their start and end apart: 2 -> 2, of which waited for: 2 -> 1; matrix products, arithmetic and copies ran while one was open for 1% -> 1% of each run, Pallas kernels for 0% -> 0%
where the time goes in v3:
time: 169 us; the launch traced here: 167 us
  Pallas kernels  148 us (88%)
  local copies, waits for them, and re-layouts  7.13 us (4%)
  starting transfers between devices  4.49 us (3%)
  between operations  3.88 us (2%)
  waiting for transfers between devices  2.18 us (1%)
    pallas_call x1, Pallas kernels, project(): pl.pallas_call(functools.partial(project_kernel, n), out_shape=jax.ShapeD...  122 us
    pallas_call x1, Pallas kernels, attend(): pl.pallas_call(functools.partial(attend_kernel, kv_heads, group), out_sha...  26.2 us
    unnamed x11, local copies, waits for them, and re-layouts  5.74 us
    ppermute x2, starting transfers between devices, passed_along(): return lax.ppermute(block, axis, route)  4.49 us
  transfers between devices with their start and end apart: 2, of which 1 were waited for; matrix products, arithmetic and copies ran while one was open for 1% of the time, Pallas kernels for 0%

profile of v3, /device:TPU:0, one launch (start us, length us, event | category | flops | bytes accessed | tf_op | source)
XLA Modules:
  0.0 167.2 jit_solution(9733284620636942807)
XLA Ops:
  0.0 1.4 fusion
  5.2 0.0 copy-start.1
  5.2 1.3 copy-done.1
  6.5 0.0 copy-start.2
  6.5 1.0 copy-done.2
  7.4 0.0 copy-start.3
  7.4 0.7 copy-done.3
  8.1 0.0 copy-start.4
  8.1 0.7 copy-done.4
  8.8 26.2 %shard_map.73 = bf16[6,24,4096]{2,1,0:T(8,128)(2,1)S(1)} custom-call(s32[6]{0:T(128)S(1)} %copy-done.4, s32[6,32]{1,0:T(8,128)S(1)} %copy-done.3, bf16[6,24,4096]{2,1,0:T(8,128)(2,1)S(1)} %copy-done.1, bf16[6,24,1024]{2,1,0:T(8,128)(2,1)S(1)} %copy-done.2, bf16[52,128,1024]{2,1,0:T(8,128)(2,1)} %pages_ref.1), custom_call_target="tpu_custom_call" | custom-call | flops 2617245696 | bytes 15990784 | tf_op jit(solution)/shard_map/pallas_call | solution.py:94
  35.0 0.1 collective-permute-start
  35.0 4.4 %collective-permute-start.1 = (bf16[24,4096]{1,0:T(8,128)(2,1)S(1)}, bf16[24,4096]{1,0:T(8,128)(2,1)S(1)}, u32[]{:S(2)}, u32[]{:S(2)}) collective-permute-start(bf16[24,4096]{1,0:T(8,128)(2,1)S(1)} %get-tuple-element.6), channel_id=1, source_target_pairs={{2,0},{4,2},{6,4},{8,6},{10,8},{12,10},{14,12},{16,14},{18,16},{20... | collective-permute-start | bytes 589832 | tf_op jit(solution)/shard_map/ppermute | solution.py:19
  39.5 1.3 iota_compare_fusion
  40.8 2.2 %collective-permute-done = bf16[24,4096]{1,0:T(8,128)(2,1)S(1)} collective-permute-done((bf16[24,4096]{1,0:T(8,128)(2,1)S(1)}, bf16[24,4096]{1,0:T(8,128)(2,1)S(1)}, u32[]{:S(2)}, u32[]{:S(2)}) %collective-permute-start) | collective-permute-done | bytes 196640 | tf_op jit(solution)/shard_map/ppermute | solution.py:19
  42.9 0.0 collective-permute-done.1
  42.9 0.0 copy-start
  42.9 0.2 select_select_fusion
  43.2 1.3 copy-done
  44.5 121.9 %shard_map.74 = bf16[2,72,2048]{2,1,0:T(8,128)(2,1)S(1)} custom-call(bf16[2,72,4096]{2,1,0:T(8,128)(2,1)S(1)} %bitcast.8, bf16[256,4096]{1,0:T(8,128)(2,1)S(1)} %copy-done), custom_call_target="tpu_custom_call" | custom-call | tf_op jit(solution)/shard_map/pallas_call | solution.py:323
  166.4 0.8 copy.9
  (1 shorter events, 0.0 us)
Async XLA Ops:
  5.2 1.3 copy-start.1
  6.5 1.0 copy-start.2
  7.4 0.7 copy-start.3
  8.1 0.7 copy-start.4
  35.0 8.0 %collective-permute-start = (bf16[24,4096]{1,0:T(8,128)(2,1)S(1)}, bf16[24,4096]{1,0:T(8,128)(2,1)S(1)}, u32[]{:S(2)}, u32[]{:S(2)}) collective-permute-start(bf16[24,4096]{1,0:T(8,128)(2,1)S(1)} %get-tuple-element.5), channel_id=1, source_target_pairs={{30,0},{0,2},{2,4},{4,6},{6,8},{8,10},{10,12},{12,14},{14,16},{16,... | collective-permute-start | bytes 589832 | tf_op jit(solution)/shard_map/ppermute | solution.py:19
  35.0 7.9 %collective-permute-start.1 = (bf16[24,4096]{1,0:T(8,128)(2,1)S(1)}, bf16[24,4096]{1,0:T(8,128)(2,1)S(1)}, u32[]{:S(2)}, u32[]{:S(2)}) collective-permute-start(bf16[24,4096]{1,0:T(8,128)(2,1)S(1)} %get-tuple-element.6), channel_id=1, source_target_pairs={{2,0},{4,2},{6,4},{8,6},{10,8},{12,10},{14,12},{16,14},{18,16},{20... | collective-permute-start | bytes 589832 | tf_op jit(solution)/shard_map/ppermute | solution.py:19
  42.9 1.6 copy-start
